TPU v7x, 32 devices: a whole 2x2x4 slice. The times are simulated.
32 devices in a mesh: parts: 32 (over z, y, x, core).
Axes of the slice: x: 2, y: 2, z: 4, core: 2. Of those that a mesh axis runs over, the one named last changes fastest.
Arguments:
- features: bfloat16 [65536, 256], P('parts'), may hold values from -32 to 32, as said below
- tile_values: bfloat16 [8192, 128, 128], P('parts'), may hold values from -0.0078125 to 0.009338379
- tile_blocks: int32 [8192, 2], P('parts'), may hold values from 0 to 23, as said below
- tile_count: int32 [32], P('parts'), may hold values from 24 to 256, as said below
- send_rows: int32 [32, 4, 256], P('parts'), may hold values from 0 to 2047, as said below
- recv_index: int32 [32, 1024], P('parts'), may hold values from 0 to 1023, as said below
- layer_weight: bfloat16 [2, 256, 256], replicated, may hold values from -0.375 to 0.375
- norm_gain: float32 [2, 256], replicated, may hold values from 0.1 to 1.9
- norm_shift: float32 [2, 256], replicated, may hold values from -3 to 3
Outputs:
- embedded: bfloat16 [65536, 256], P('parts')
Inputs may be any that keep to these rules, and one draw needn't show every extreme that they name: `features`: every entry is finite. `tile_blocks`: column 0 is a row block (0 to 15), column 1 a column block of columns_l. A device's first 16 tiles are the diagonal blocks (t, t) in order; the next 8 tiles have the column blocks 2048 // 128, 17, ... in order; blocks may repeat. `tile_count`: the live tiles are the leading ones of a device's list; some device has all 256 live in every draw. `send_rows`: entry [q, n] lists 256 distinct local rows that device q sends to device q + o[n], o = (1, -1, 2, -2). `recv_index`: each device's row is a permutation.
All inputs are finite; a program needn't handle non-finite values.
Results may differ from a plain program's by a relative error of at most 0.0072.
Values may be sent and summed in bfloat16 or wider, within the bound.
A program may use at most 64 MiB of HBM per device.

v0:
```python
import math

import jax
import jax.numpy as jnp
from jax import lax
from jax.sharding import PartitionSpec as P

neighbour_offsets = (1, -1, 2, -2)
norm_eps = 1e-05
tile_group = 32


def shifted(value, axis, steps):
    count = lax.axis_size(axis)
    first, last = (max(0, -steps), min(count, count - steps))
    return lax.ppermute(value, axis, [(source, source + steps) for source in range(first, last)])


def fetch_halo(own_rows, send_rows, recv_index):
    pieces = []
    for position, offset in enumerate(neighbour_offsets):
        outgoing = jnp.take(own_rows, send_rows[0, position], axis=0)
        pieces.append(shifted(outgoing, "parts", offset))
    received = jnp.concatenate(pieces, axis=0)
    return jnp.take(received, recv_index[0], axis=0)


def owned_sum(values, blocks, first_tile, live_count, row_count, column_blocks):
    picked = jnp.take(column_blocks, blocks[:, 1], axis=0)
    partial_value = jnp.einsum("tij,tjc->tic", values, picked, preferred_element_type=jnp.float32)
    tile_number = first_tile + jnp.arange(values.shape[0], dtype=jnp.int32)
    live = tile_number < live_count
    owners = (blocks[:, 0][None, :] == jnp.arange(row_count, dtype=jnp.int32)[:, None]) & live[
        None, :
    ]
    return jnp.einsum(
        "rt,tic->ric", owners.astype(jnp.float32), partial_value, precision=lax.Precision.HIGHEST
    )


def aggregate(columns, row_count, tile_values, tile_blocks, live_count):
    tile_edge = tile_values.shape[1]
    channels = columns.shape[1]
    column_blocks = columns.reshape(-1, tile_edge, channels)
    group_size = math.gcd(tile_values.shape[0], tile_group)
    turn_count = tile_values.shape[0] // group_size

    def one_group(counter, carried):
        first_tile = counter * group_size
        values = lax.dynamic_slice_in_dim(tile_values, first_tile, group_size, 0)
        blocks = lax.dynamic_slice_in_dim(tile_blocks, first_tile, group_size, 0)
        return carried + owned_sum(values, blocks, first_tile, live_count, row_count, column_blocks)

    summed = lax.fori_loop(
        0, turn_count, one_group, jnp.zeros((row_count, tile_edge, channels), jnp.float32)
    )
    return summed.reshape(row_count * tile_edge, channels)


def transform(own_rows, halo_block, tile_values, tile_blocks, live_count, weight):
    row_count = own_rows.shape[0] // tile_values.shape[1]
    columns = jnp.concatenate([own_rows, halo_block], axis=0)
    summed = aggregate(columns, row_count, tile_values, tile_blocks, live_count)
    return jnp.dot(summed.astype(jnp.bfloat16), weight, preferred_element_type=jnp.float32).astype(
        jnp.bfloat16
    )


def moments(mixed_rows):
    widened = mixed_rows.astype(jnp.float32)
    vertex_total = mixed_rows.shape[0] * lax.axis_size("parts")
    column_sums, squares = lax.psum(
        (jnp.sum(widened, axis=0), jnp.sum(jnp.square(widened), axis=0)), "parts"
    )
    centre = column_sums / vertex_total
    spread = squares / vertex_total - jnp.square(centre)
    return (centre, spread)


def normalise(mixed_rows, centre, spread, gain_row, shift_row):
    widened = mixed_rows.astype(jnp.float32)
    scaled = (widened - centre) / jnp.sqrt(spread + norm_eps)
    return jax.nn.relu(gain_row * scaled + shift_row).astype(jnp.bfloat16)


def shards(
    features,
    tile_values,
    tile_blocks,
    tile_count,
    send_rows,
    recv_index,
    layer_weight,
    norm_gain,
    norm_shift,
):
    live_count = tile_count[0]
    halo_block = fetch_halo(features, send_rows, recv_index)
    first_mixed = transform(
        features, halo_block, tile_values, tile_blocks, live_count, layer_weight[0]
    )
    centre, spread = moments(first_mixed)
    hidden = normalise(first_mixed, centre, spread, norm_gain[0], norm_shift[0])
    second_halo = fetch_halo(hidden, send_rows, recv_index)
    second_mixed = transform(
        hidden, second_halo, tile_values, tile_blocks, live_count, layer_weight[1]
    )
    centre, spread = moments(second_mixed)
    return normalise(second_mixed, centre, spread, norm_gain[1], norm_shift[1])


def solution(mesh):
    return jax.shard_map(
        shards,
        mesh=mesh,
        in_specs=(
            P("parts", None),
            P("parts", None, None),
            P("parts", None),
            P("parts"),
            P("parts", None, None),
            P("parts", None),
            P(),
            P(),
            P(),
        ),
        out_specs=P("parts", None),
        check_vma=False,
    )
```

profile of v0, /device:TPU:0, one launch (start us, length us, event | category | flops | bytes accessed | tf_op | source)
XLA Modules:
  0.0 386.9 jit_solution(17864943791084396211)
XLA Ops:
  9.7 6.7 %collective-permute-start.2 = (bf16[256,256]{1,0:T(8,128)(2,1)S(1)}, bf16[256,256]{1,0:T(8,128)(2,1)S(1)}, u32[]{:S(2)}, u32[]{:S(2)}) collective-permute-start(bf16[256,256]{1,0:T(8,128)(2,1)S(1)} %broadcast_select_fusion.5), channel_id=1, source_target_pairs={{0,2},{1,3},{2,4},{3,5},{4,6},{5,7},{6,8},{7,9},{8,10},{9,11},{10,... | collective-permute-start | bytes 393224 | tf_op jit(solution)/shard_map/ppermute | solution.py:16
  19.8 5.2 %collective-permute-done.3 = bf16[256,256]{1,0:T(8,128)(2,1)S(1)} collective-permute-done((bf16[256,256]{1,0:T(8,128)(2,1)S(1)}, bf16[256,256]{1,0:T(8,128)(2,1)S(1)}, u32[]{:S(2)}, u32[]{:S(2)}) %collective-permute-start.3) | collective-permute-done | bytes 131104 | tf_op jit(solution)/shard_map/ppermute | solution.py:16
  30.4 117.5 %while.28 = (s32[]{:T(128)}, f32[16,128,256]{2,0,1:T(8,128)}, s32[256,2]{0,1:T(2,128)S(1)}, s32[]{:T(128)}, bf16[256,128,128]{2,1,0:T(8,128)(2,1)}, /*index=5*/b...) while((s32[]{:T(128)}, f32[16,128,256]{2,0,1:T(8,128)}, ...), condition=%wide.region_1.0_spmd.clone, body=%wide.region_0.4_spmd.clone.sunk | while | flops 471861504 | bytes 19928748 | solution.py:54
  37.2 7.3 %select_add_fusion.4 = f32[16,128,256]{2,0,1:T(8,128)} fusion(f32[16,128,256]{2,0,1:T(8,128)} %get-tuple-element.413, f32[32,128,256]{2,1,0:T(8,128)} %fusion.68, pred[]{:T(512)S(6)} %compare.6, s32[32]{0:T(128)S(1)} %slice_bitcast_fusion.4, pred[32]{0:T(512)(128)(4,1)S(1)} %add_compare_fusion.4), kind=kOutput, calls=%fused_computation.16.clone.1 | convolution fusion | flops 202376192 | bytes 8388769 | tf_op jit(solution)/shard_map/while/body/eval_jaxpr/rt,tic->ric/dot_general | solution.py:36
  51.3 8.0 %select_add_fusion.4 = f32[16,128,256]{2,0,1:T(8,128)} fusion(f32[16,128,256]{2,0,1:T(8,128)} %get-tuple-element.413, f32[32,128,256]{2,1,0:T(8,128)} %fusion.68, pred[]{:T(512)S(6)} %compare.6, s32[32]{0:T(128)S(1)} %slice_bitcast_fusion.4, pred[32]{0:T(512)(128)(4,1)S(1)} %add_compare_fusion.4), kind=kOutput, calls=%fused_computation.16.clone.1 | convolution fusion | flops 202376192 | bytes 8388769 | tf_op jit(solution)/shard_map/while/body/eval_jaxpr/rt,tic->ric/dot_general | solution.py:36
  66.1 8.0 %select_add_fusion.4 = f32[16,128,256]{2,0,1:T(8,128)} fusion(f32[16,128,256]{2,0,1:T(8,128)} %get-tuple-element.413, f32[32,128,256]{2,1,0:T(8,128)} %fusion.68, pred[]{:T(512)S(6)} %compare.6, s32[32]{0:T(128)S(1)} %slice_bitcast_fusion.4, pred[32]{0:T(512)(128)(4,1)S(1)} %add_compare_fusion.4), kind=kOutput, calls=%fused_computation.16.clone.1 | convolution fusion | flops 202376192 | bytes 8388769 | tf_op jit(solution)/shard_map/while/body/eval_jaxpr/rt,tic->ric/dot_general | solution.py:36
  80.9 8.0 %select_add_fusion.4 = f32[16,128,256]{2,0,1:T(8,128)} fusion(f32[16,128,256]{2,0,1:T(8,128)} %get-tuple-element.413, f32[32,128,256]{2,1,0:T(8,128)} %fusion.68, pred[]{:T(512)S(6)} %compare.6, s32[32]{0:T(128)S(1)} %slice_bitcast_fusion.4, pred[32]{0:T(512)(128)(4,1)S(1)} %add_compare_fusion.4), kind=kOutput, calls=%fused_computation.16.clone.1 | convolution fusion | flops 202376192 | bytes 8388769 | tf_op jit(solution)/shard_map/while/body/eval_jaxpr/rt,tic->ric/dot_general | solution.py:36
  95.6 8.0 %select_add_fusion.4 = f32[16,128,256]{2,0,1:T(8,128)} fusion(f32[16,128,256]{2,0,1:T(8,128)} %get-tuple-element.413, f32[32,128,256]{2,1,0:T(8,128)} %fusion.68, pred[]{:T(512)S(6)} %compare.6, s32[32]{0:T(128)S(1)} %slice_bitcast_fusion.4, pred[32]{0:T(512)(128)(4,1)S(1)} %add_compare_fusion.4), kind=kOutput, calls=%fused_computation.16.clone.1 | convolution fusion | flops 202376192 | bytes 8388769 | tf_op jit(solution)/shard_map/while/body/eval_jaxpr/rt,tic->ric/dot_general | solution.py:36
  110.4 8.0 %select_add_fusion.4 = f32[16,128,256]{2,0,1:T(8,128)} fusion(f32[16,128,256]{2,0,1:T(8,128)} %get-tuple-element.413, f32[32,128,256]{2,1,0:T(8,128)} %fusion.68, pred[]{:T(512)S(6)} %compare.6, s32[32]{0:T(128)S(1)} %slice_bitcast_fusion.4, pred[32]{0:T(512)(128)(4,1)S(1)} %add_compare_fusion.4), kind=kOutput, calls=%fused_computation.16.clone.1 | convolution fusion | flops 202376192 | bytes 8388769 | tf_op jit(solution)/shard_map/while/body/eval_jaxpr/rt,tic->ric/dot_general | solution.py:36
  125.2 8.0 %select_add_fusion.4 = f32[16,128,256]{2,0,1:T(8,128)} fusion(f32[16,128,256]{2,0,1:T(8,128)} %get-tuple-element.413, f32[32,128,256]{2,1,0:T(8,128)} %fusion.68, pred[]{:T(512)S(6)} %compare.6, s32[32]{0:T(128)S(1)} %slice_bitcast_fusion.4, pred[32]{0:T(512)(128)(4,1)S(1)} %add_compare_fusion.4), kind=kOutput, calls=%fused_computation.16.clone.1 | convolution fusion | flops 202376192 | bytes 8388769 | tf_op jit(solution)/shard_map/while/body/eval_jaxpr/rt,tic->ric/dot_general | solution.py:36
  140.0 8.0 %select_add_fusion.4 = f32[16,128,256]{2,0,1:T(8,128)} fusion(f32[16,128,256]{2,0,1:T(8,128)} %get-tuple-element.413, f32[32,128,256]{2,1,0:T(8,128)} %fusion.68, pred[]{:T(512)S(6)} %compare.6, s32[32]{0:T(128)S(1)} %slice_bitcast_fusion.4, pred[32]{0:T(512)(128)(4,1)S(1)} %add_compare_fusion.4), kind=kOutput, calls=%fused_computation.16.clone.1 | convolution fusion | flops 202376192 | bytes 8388769 | tf_op jit(solution)/shard_map/while/body/eval_jaxpr/rt,tic->ric/dot_general | solution.py:36
  151.3 43.9 %all-reduce.1 = (f32[256]{0:T(256)S(1)}, f32[256]{0:T(256)S(1)}) all-reduce(f32[256]{0:T(256)S(1)} %get-tuple-element.273, f32[256]{0:T(256)S(1)} %get-tuple-element.272), channel_id=1, replica_groups=mesh['parts'=32] {'parts'}, use_global_device_ids=true, to_apply=%region_5.9 | all-reduce | flops 512 | bytes 4096 | tf_op jit(solution)/shard_map/psum | solution.py:72
  203.1 7.2 %collective-permute-start.6 = (bf16[256,256]{1,0:T(8,128)(2,1)S(1)}, bf16[256,256]{1,0:T(8,128)(2,1)S(1)}, u32[]{:S(2)}, u32[]{:S(2)}) collective-permute-start(bf16[256,256]{1,0:T(8,128)(2,1)S(1)} %broadcast_select_fusion.4), channel_id=1, source_target_pairs={{0,2},{1,3},{2,4},{3,5},{4,6},{5,7},{6,8},{7,9},{8,10},{9,11},{10,... | collective-permute-start | bytes 393224 | tf_op jit(solution)/shard_map/ppermute | solution.py:16
  213.0 5.3 %collective-permute-done.7 = bf16[256,256]{1,0:T(8,128)(2,1)S(1)} collective-permute-done((bf16[256,256]{1,0:T(8,128)(2,1)S(1)}, bf16[256,256]{1,0:T(8,128)(2,1)S(1)}, u32[]{:S(2)}, u32[]{:S(2)}) %collective-permute-start.7) | collective-permute-done | bytes 131104 | tf_op jit(solution)/shard_map/ppermute | solution.py:16
  223.8 117.5 %while.29 = (s32[]{:T(128)}, f32[16,128,256]{2,0,1:T(8,128)}, s32[256,2]{0,1:T(2,128)S(1)}, s32[]{:T(128)}, bf16[256,128,128]{2,1,0:T(8,128)(2,1)}, /*index=5*/b...) while((s32[]{:T(128)}, f32[16,128,256]{2,0,1:T(8,128)}, ...), condition=%wide.region_7.11_spmd.clone, body=%wide.region_6.10_spmd.clone.sunk | while | flops 471861504 | bytes 19928748 | solution.py:54
  230.6 7.3 %select_add_fusion.5 = f32[16,128,256]{2,0,1:T(8,128)} fusion(f32[16,128,256]{2,0,1:T(8,128)} %get-tuple-element.443, f32[32,128,256]{2,1,0:T(8,128)} %fusion.73, pred[]{:T(512)S(6)} %compare.7, s32[32]{0:T(128)S(1)} %slice_bitcast_fusion.5, pred[32]{0:T(512)(128)(4,1)S(1)} %add_compare_fusion.5), kind=kOutput, calls=%fused_computation.37.clone.1 | convolution fusion | flops 202376192 | bytes 8388769 | tf_op jit(solution)/shard_map/while/body/eval_jaxpr/rt,tic->ric/dot_general | solution.py:36
  244.7 8.0 %select_add_fusion.5 = f32[16,128,256]{2,0,1:T(8,128)} fusion(f32[16,128,256]{2,0,1:T(8,128)} %get-tuple-element.443, f32[32,128,256]{2,1,0:T(8,128)} %fusion.73, pred[]{:T(512)S(6)} %compare.7, s32[32]{0:T(128)S(1)} %slice_bitcast_fusion.5, pred[32]{0:T(512)(128)(4,1)S(1)} %add_compare_fusion.5), kind=kOutput, calls=%fused_computation.37.clone.1 | convolution fusion | flops 202376192 | bytes 8388769 | tf_op jit(solution)/shard_map/while/body/eval_jaxpr/rt,tic->ric/dot_general | solution.py:36
  259.5 8.0 %select_add_fusion.5 = f32[16,128,256]{2,0,1:T(8,128)} fusion(f32[16,128,256]{2,0,1:T(8,128)} %get-tuple-element.443, f32[32,128,256]{2,1,0:T(8,128)} %fusion.73, pred[]{:T(512)S(6)} %compare.7, s32[32]{0:T(128)S(1)} %slice_bitcast_fusion.5, pred[32]{0:T(512)(128)(4,1)S(1)} %add_compare_fusion.5), kind=kOutput, calls=%fused_computation.37.clone.1 | convolution fusion | flops 202376192 | bytes 8388769 | tf_op jit(solution)/shard_map/while/body/eval_jaxpr/rt,tic->ric/dot_general | solution.py:36
  274.3 8.0 %select_add_fusion.5 = f32[16,128,256]{2,0,1:T(8,128)} fusion(f32[16,128,256]{2,0,1:T(8,128)} %get-tuple-element.443, f32[32,128,256]{2,1,0:T(8,128)} %fusion.73, pred[]{:T(512)S(6)} %compare.7, s32[32]{0:T(128)S(1)} %slice_bitcast_fusion.5, pred[32]{0:T(512)(128)(4,1)S(1)} %add_compare_fusion.5), kind=kOutput, calls=%fused_computation.37.clone.1 | convolution fusion | flops 202376192 | bytes 8388769 | tf_op jit(solution)/shard_map/while/body/eval_jaxpr/rt,tic->ric/dot_general | solution.py:36
  289.0 8.0 %select_add_fusion.5 = f32[16,128,256]{2,0,1:T(8,128)} fusion(f32[16,128,256]{2,0,1:T(8,128)} %get-tuple-element.443, f32[32,128,256]{2,1,0:T(8,128)} %fusion.73, pred[]{:T(512)S(6)} %compare.7, s32[32]{0:T(128)S(1)} %slice_bitcast_fusion.5, pred[32]{0:T(512)(128)(4,1)S(1)} %add_compare_fusion.5), kind=kOutput, calls=%fused_computation.37.clone.1 | convolution fusion | flops 202376192 | bytes 8388769 | tf_op jit(solution)/shard_map/while/body/eval_jaxpr/rt,tic->ric/dot_general | solution.py:36
  303.8 8.0 %select_add_fusion.5 = f32[16,128,256]{2,0,1:T(8,128)} fusion(f32[16,128,256]{2,0,1:T(8,128)} %get-tuple-element.443, f32[32,128,256]{2,1,0:T(8,128)} %fusion.73, pred[]{:T(512)S(6)} %compare.7, s32[32]{0:T(128)S(1)} %slice_bitcast_fusion.5, pred[32]{0:T(512)(128)(4,1)S(1)} %add_compare_fusion.5), kind=kOutput, calls=%fused_computation.37.clone.1 | convolution fusion | flops 202376192 | bytes 8388769 | tf_op jit(solution)/shard_map/while/body/eval_jaxpr/rt,tic->ric/dot_general | solution.py:36
  318.6 8.0 %select_add_fusion.5 = f32[16,128,256]{2,0,1:T(8,128)} fusion(f32[16,128,256]{2,0,1:T(8,128)} %get-tuple-element.443, f32[32,128,256]{2,1,0:T(8,128)} %fusion.73, pred[]{:T(512)S(6)} %compare.7, s32[32]{0:T(128)S(1)} %slice_bitcast_fusion.5, pred[32]{0:T(512)(128)(4,1)S(1)} %add_compare_fusion.5), kind=kOutput, calls=%fused_computation.37.clone.1 | convolution fusion | flops 202376192 | bytes 8388769 | tf_op jit(solution)/shard_map/while/body/eval_jaxpr/rt,tic->ric/dot_general | solution.py:36
  333.4 8.0 %select_add_fusion.5 = f32[16,128,256]{2,0,1:T(8,128)} fusion(f32[16,128,256]{2,0,1:T(8,128)} %get-tuple-element.443, f32[32,128,256]{2,1,0:T(8,128)} %fusion.73, pred[]{:T(512)S(6)} %compare.7, s32[32]{0:T(128)S(1)} %slice_bitcast_fusion.5, pred[32]{0:T(512)(128)(4,1)S(1)} %add_compare_fusion.5), kind=kOutput, calls=%fused_computation.37.clone.1 | convolution fusion | flops 202376192 | bytes 8388769 | tf_op jit(solution)/shard_map/while/body/eval_jaxpr/rt,tic->ric/dot_general | solution.py:36
  344.6 40.8 %all-reduce = (f32[256]{0:T(256)S(1)}, f32[256]{0:T(256)S(1)}) all-reduce(f32[256]{0:T(256)S(1)} %get-tuple-element.271, f32[256]{0:T(256)S(1)} %get-tuple-element.270), channel_id=1, replica_groups=mesh['parts'=32] {'parts'}, use_global_device_ids=true, to_apply=%region_11.15 | all-reduce | flops 512 | bytes 4096 | tf_op jit(solution)/shard_map/psum | solution.py:72
  (187 shorter events, 151.0 us)
Async XLA Ops:
  0.0 5.8 %copy-start = (bf16[2048,256]{1,0:T(8,128)(2,1)S(1)}, bf16[2048,256]{1,0:T(8,128)(2,1)}, u32[]{:S(2)}) copy-start(bf16[2048,256]{1,0:T(8,128)(2,1)} %param.19) | copy-start | bytes 3145732
  3.3 15.8 %collective-permute-start = (bf16[256,256]{1,0:T(8,128)(2,1)S(1)}, bf16[256,256]{1,0:T(8,128)(2,1)S(1)}, u32[]{:S(2)}, u32[]{:S(2)}) collective-permute-start(bf16[256,256]{1,0:T(8,128)(2,1)S(1)} %broadcast_select_fusion.9), channel_id=1, source_target_pairs={{0,1},{1,2},{2,3},{3,4},{4,5},{5,6},{6,7},{7,8},{8,9},{9,10},{10,1... | collective-permute-start | bytes 393224 | tf_op jit(solution)/shard_map/ppermute | solution.py:16
  5.8 13.3 %copy-start.2 = (s32[1,1024]{1,0:T(1,128)S(1)}, s32[1,1024]{1,0:T(1,128)}, u32[]{:S(2)}) copy-start(s32[1,1024]{1,0:T(1,128)} %param.24) | copy-start | bytes 12292
  5.8 13.3 %copy-start.3 = (f32[2,256]{1,0:T(2,128)S(1)}, f32[2,256]{1,0:T(2,128)}, u32[]{:S(2)}) copy-start(f32[2,256]{1,0:T(2,128)} %param.27) | copy-start | bytes 6148
  5.8 13.3 %copy-start.4 = (f32[2,256]{1,0:T(2,128)S(1)}, f32[2,256]{1,0:T(2,128)}, u32[]{:S(2)}) copy-start(f32[2,256]{1,0:T(2,128)} %param.26) | copy-start | bytes 6148
  7.1 12.1 %collective-permute-start.1 = (bf16[256,256]{1,0:T(8,128)(2,1)S(1)}, bf16[256,256]{1,0:T(8,128)(2,1)S(1)}, u32[]{:S(2)}, u32[]{:S(2)}) collective-permute-start(bf16[256,256]{1,0:T(8,128)(2,1)S(1)} %broadcast_select_fusion.7), channel_id=1, source_target_pairs={{1,0},{2,1},{3,2},{4,3},{5,4},{6,5},{7,6},{8,7},{9,8},{10,9},{11,1... | collective-permute-start | bytes 393224 | tf_op jit(solution)/shard_map/ppermute | solution.py:16
  9.7 10.1 %collective-permute-start.2 = (bf16[256,256]{1,0:T(8,128)(2,1)S(1)}, bf16[256,256]{1,0:T(8,128)(2,1)S(1)}, u32[]{:S(2)}, u32[]{:S(2)}) collective-permute-start(bf16[256,256]{1,0:T(8,128)(2,1)S(1)} %broadcast_select_fusion.5), channel_id=1, source_target_pairs={{0,2},{1,3},{2,4},{3,5},{4,6},{5,7},{6,8},{7,9},{8,10},{9,11},{10,... | collective-permute-start | bytes 393224 | tf_op jit(solution)/shard_map/ppermute | solution.py:16
  17.7 7.2 %collective-permute-start.3 = (bf16[256,256]{1,0:T(8,128)(2,1)S(1)}, bf16[256,256]{1,0:T(8,128)(2,1)S(1)}, u32[]{:S(2)}, u32[]{:S(2)}) collective-permute-start(bf16[256,256]{1,0:T(8,128)(2,1)S(1)} %broadcast_select_fusion.3), channel_id=1, source_target_pairs={{2,0},{3,1},{4,2},{5,3},{6,4},{7,5},{8,6},{9,7},{10,8},{11,9},{12,... | collective-permute-start | bytes 393224 | tf_op jit(solution)/shard_map/ppermute | solution.py:16
  29.0 1.5 copy-start.1
  147.9 2.8 copy-start.5
  200.3 11.4 %collective-permute-start.4 = (bf16[256,256]{1,0:T(8,128)(2,1)S(1)}, bf16[256,256]{1,0:T(8,128)(2,1)S(1)}, u32[]{:S(2)}, u32[]{:S(2)}) collective-permute-start(bf16[256,256]{1,0:T(8,128)(2,1)S(1)} %broadcast_select_fusion.8), channel_id=1, source_target_pairs={{0,1},{1,2},{2,3},{3,4},{4,5},{5,6},{6,7},{7,8},{8,9},{9,10},{10,1... | collective-permute-start | bytes 393224 | tf_op jit(solution)/shard_map/ppermute | solution.py:16
  201.7 10.0 %collective-permute-start.5 = (bf16[256,256]{1,0:T(8,128)(2,1)S(1)}, bf16[256,256]{1,0:T(8,128)(2,1)S(1)}, u32[]{:S(2)}, u32[]{:S(2)}) collective-permute-start(bf16[256,256]{1,0:T(8,128)(2,1)S(1)} %broadcast_select_fusion.6), channel_id=1, source_target_pairs={{1,0},{2,1},{3,2},{4,3},{5,4},{6,5},{7,6},{8,7},{9,8},{10,9},{11,1... | collective-permute-start | bytes 393224 | tf_op jit(solution)/shard_map/ppermute | solution.py:16
  203.1 9.9 %collective-permute-start.6 = (bf16[256,256]{1,0:T(8,128)(2,1)S(1)}, bf16[256,256]{1,0:T(8,128)(2,1)S(1)}, u32[]{:S(2)}, u32[]{:S(2)}) collective-permute-start(bf16[256,256]{1,0:T(8,128)(2,1)S(1)} %broadcast_select_fusion.4), channel_id=1, source_target_pairs={{0,2},{1,3},{2,4},{3,5},{4,6},{5,7},{6,8},{7,9},{8,10},{9,11},{10,... | collective-permute-start | bytes 393224 | tf_op jit(solution)/shard_map/ppermute | solution.py:16
  210.4 8.0 %collective-permute-start.7 = (bf16[256,256]{1,0:T(8,128)(2,1)S(1)}, bf16[256,256]{1,0:T(8,128)(2,1)S(1)}, u32[]{:S(2)}, u32[]{:S(2)}) collective-permute-start(bf16[256,256]{1,0:T(8,128)(2,1)S(1)} %broadcast_select_fusion.2), channel_id=1, source_target_pairs={{2,0},{3,1},{4,2},{5,3},{6,4},{7,5},{8,6},{9,7},{10,8},{11,9},{12,... | collective-permute-start | bytes 393224 | tf_op jit(solution)/shard_map/ppermute | solution.py:16
where the time goes:
time: 389 us; the launch traced here: 387 us
  matrix products  190 us (49%)
  blocking collectives  84.7 us (22%)
  local copies, waits for them, and re-layouts  59.2 us (15%)
  starting transfers between devices  22.8 us (6%)
  other arithmetic  16.5 us (4%)
  waiting for transfers between devices  12.5 us (3%)
    dot_general x16, matrix products, owned_sum(): jnp.einsum('rt,tic->ric', owners.astype(jnp.float32), partial_value, prec...  126 us
    psum x2, blocking collectives, moments(): lax.psum((jnp.sum(widened, axis=0), jnp.sum(jnp.square(widened), axis=0))...  84.7 us
    dot_general x16, matrix products, owned_sum(): jnp.einsum('tij,tjc->tic', values, picked, preferred_element_type=jnp.flo...  63.4 us
    gather x16, local copies, waits for them, and re-layouts, owned_sum(): picked = jnp.take(column_blocks, blocks[:, 1], axis=0)  33.4 us
    ppermute x8, starting transfers between devices, shifted(): lax.ppermute(value, axis, [(source, source + steps) for source in range(f...  22.8 us
    ppermute x8, waiting for transfers between devices, shifted(): lax.ppermute(value, axis, [(source, source + steps) for source in range(f...  12.5 us
    lt x16, other arithmetic, owned_sum(): live = tile_number < live_count  10.4 us
    gather x8, local copies, waits for them, and re-layouts, fetch_halo(): outgoing = jnp.take(own_rows, send_rows[0, position], axis=0)  10.4 us
  transfers between devices with their start and end apart: 8, of which 4 were waited for; matrix products, arithmetic and copies ran while one was open for 1% of the time, Pallas kernels for 0%

commit v1 on v0

v1 whole, which is shorter than its diff:
```python
import functools

import jax
import jax.numpy as jnp
from jax import lax
from jax.experimental import pallas as pl
from jax.experimental.pallas import tpu as pltpu
from jax.sharding import PartitionSpec as P

neighbour_offsets = (1, -1, 2, -2)
norm_eps = 1e-05
MESH = pl.DeviceIdType.MESH


def plan(tile_blocks, live_count, row_count, group_total):
    tile_total = tile_blocks.shape[0]
    number = jnp.arange(tile_total, dtype=jnp.int32)
    live = number < live_count
    rows = jnp.where(live, tile_blocks[:, 0], row_count)
    same = rows[:, None] == rows[None, :]
    rank = jnp.sum((same & (number[None, :] < number[:, None])).astype(jnp.int32), axis=1)
    blocks = jnp.arange(row_count, dtype=jnp.int32)
    counts = jnp.sum((rows[None, :] == blocks[:, None]).astype(jnp.int32), axis=1)
    groups = (counts + 1) // 2
    start = jnp.sum(jnp.where(blocks[None, :] < blocks[:, None], groups[None, :], 0), axis=1)
    first = jnp.sum(jnp.where(rows[:, None] == blocks[None, :], start[None, :], 0), axis=1)
    slot = jnp.where(live, 2 * first + rank, -1)
    hit = jnp.arange(2 * group_total, dtype=jnp.int32)[:, None] == slot[None, :]
    tile_of = tile_total + jnp.sum(jnp.where(hit, number[None, :] - tile_total, 0), axis=1)
    column_of = jnp.sum(jnp.where(hit, tile_blocks[:, 1][None, :], 0), axis=1)
    group_number = jnp.arange(group_total, dtype=jnp.int32)
    keep = 1.0 - jnp.sum((group_number[:, None] == start[None, :]).astype(jnp.float32), axis=1)
    return tile_of, column_of, keep, start + groups - 1


def kernel(
    n,
    tile_of,
    column_of,
    keep,
    last_of,
    send_rows,
    recv_index,
    weight,
    gain,
    shift,
    features,
    tile_values,
    out,
    tiles,
    columns,
    pick,
    order,
    run,
    mixed,
    outgoing,
    received,
    stats,
    tile_sem,
    feature_sem,
    out_sem,
    halo_send,
    halo_recv,
    stat_send,
    stat_recv,
):
    me = lax.axis_index("parts")
    layers = weight.shape[0]
    tile_total, edge, _ = tile_values.shape
    row_count, _, channels = out.shape
    vertices = row_count * edge
    halo_count = received.shape[2]
    group_total = keep.shape[0]
    neighbours = len(neighbour_offsets)

    feature_copy = pltpu.make_async_copy(features, columns.at[pl.ds(0, row_count)], feature_sem)
    feature_copy.start()
    tile_copy = pltpu.make_async_copy(tile_values, tiles.at[pl.ds(0, tile_total)], tile_sem)
    tile_copy.start()

    barrier = pltpu.get_barrier_semaphore()

    def greet(step, carry):
        pl.semaphore_signal(
            barrier, inc=1, device_id=(lax.rem(me + step, n),), device_id_type=MESH
        )
        return carry

    lax.fori_loop(1, n, greet, 0)

    tiles[tile_total] = jnp.zeros((edge, tiles.shape[2]), tiles.dtype)
    for position, offset in enumerate(neighbour_offsets):
        source = me - offset

        @pl.when((source < 0) | (source >= n))
        def _():
            for layer in range(layers):
                received[layer, position] = jnp.zeros((halo_count, channels), received.dtype)

    lane = lax.broadcasted_iota(jnp.int32, (128, 128), 1)

    def one_hot(index_row, target, first_row, width):
        spread = jnp.broadcast_to(index_row, (128, 128)).T
        for chunk in range(width // 128):
            found = spread == lane + chunk * 128
            target[pl.ds(first_row, 128), pl.ds(chunk * 128, 128)] = jnp.where(
                found, 1.0, 0.0
            ).astype(jnp.bfloat16)

    for position in range(neighbours):
        for half in range(halo_count // 128):
            one_hot(
                send_rows[0, pl.ds(position, 1), pl.ds(half * 128, 128)],
                pick,
                position * halo_count + half * 128,
                vertices,
            )
    feature_copy.wait()

    def halo_copy(layer, position, device):
        return pltpu.make_async_remote_copy(
            src_ref=outgoing.at[layer, position],
            dst_ref=received.at[layer, position],
            send_sem=halo_send.at[layer, position],
            recv_sem=halo_recv.at[layer, position],
            device_id=(device,),
            device_id_type=MESH,
        )

    def stat_copy(layer, step, device):
        return pltpu.make_async_remote_copy(
            src_ref=stats.at[layer, me],
            dst_ref=stats.at[layer, me],
            send_sem=stat_send.at[layer, step],
            recv_sem=stat_recv.at[layer, step],
            device_id=(device,),
            device_id_type=MESH,
        )

    for layer in range(layers):
        for position, offset in enumerate(neighbour_offsets):
            outgoing[layer, position] = jnp.dot(
                pick[pl.ds(position * halo_count, halo_count), :],
                columns[pl.ds(0, row_count)].reshape(vertices, channels),
                preferred_element_type=jnp.float32,
            ).astype(jnp.bfloat16)
        if layer == 0:
            pl.semaphore_wait(barrier, n - 1)
        for position, offset in enumerate(neighbour_offsets):
            target = me + offset

            @pl.when((target >= 0) & (target < n))
            def _():
                halo_copy(layer, position, target).start()

        if layer == 0:
            for part in range(neighbours * halo_count // 128):
                one_hot(
                    recv_index[pl.ds(0, 1), pl.ds(part * 128, 128)],
                    order,
                    part * 128,
                    neighbours * halo_count,
                )
        for position, offset in enumerate(neighbour_offsets):
            source = me - offset

            @pl.when((source >= 0) & (source < n))
            def _():
                halo_copy(layer, position, me).wait_recv()

        arrived = received[layer].reshape(neighbours * halo_count, channels)
        columns[pl.ds(row_count, neighbours * halo_count // edge)] = (
            jnp.dot(order[...], arrived, preferred_element_type=jnp.float32)
            .astype(jnp.bfloat16)
            .reshape(neighbours * halo_count // edge, edge, channels)
        )
        if layer == 0:
            tile_copy.wait()

        unroll = 4 if group_total % 4 == 0 else 1

        def sweep(turn, total):
            for step in range(unroll):
                group = turn * unroll + step
                values = jnp.concatenate(
                    [tiles[tile_of[2 * group]], tiles[tile_of[2 * group + 1]]], axis=1
                )
                picked = [columns[column_of[2 * group + k]] for k in range(2)]
                total = total * keep[group] + jnp.dot(
                    values, jnp.concatenate(picked, axis=0), preferred_element_type=jnp.float32
                )
                run[group] = total.astype(jnp.bfloat16)
            return total

        lax.fori_loop(
            0, group_total // unroll, sweep, jnp.zeros((edge, channels), jnp.float32)
        )

        def mix(block, carry):
            sums, squares = carry
            product = jnp.dot(
                run[last_of[block]], weight[layer], preferred_element_type=jnp.float32
            ).astype(jnp.bfloat16)
            mixed[block] = product
            wide = product.astype(jnp.float32).reshape(edge // 8, 8, channels)
            return sums + jnp.sum(wide, axis=0), squares + jnp.sum(wide * wide, axis=0)

        nothing = jnp.zeros((8, channels), jnp.float32)
        sums, squares = lax.fori_loop(0, row_count, mix, (nothing, nothing))
        stats[layer, me] = jnp.concatenate(
            [jnp.sum(sums, axis=0, keepdims=True), jnp.sum(squares, axis=0, keepdims=True)], axis=0
        )

        def share(step, carry):
            stat_copy(layer, step, lax.rem(me + step, n)).start()
            return carry

        lax.fori_loop(1, n, share, 0)

        for position, offset in enumerate(neighbour_offsets):
            target = me + offset

            @pl.when((target >= 0) & (target < n))
            def _():
                halo_copy(layer, position, target).wait_send()

        def collect(step, carry):
            pltpu.make_async_remote_copy(
                src_ref=stats.at[layer, me],
                dst_ref=stats.at[layer, lax.rem(me + n - step, n)],
                send_sem=stat_send.at[layer, step],
                recv_sem=stat_recv.at[layer, step],
                device_id=(lax.rem(me + step, n),),
                device_id_type=MESH,
            ).wait()
            return carry

        lax.fori_loop(1, n, collect, 0)
        both = jnp.sum(stats[layer], axis=0) / (vertices * n)
        centre = both[0:1]
        spread = jnp.maximum(both[1:2] - centre * centre, 0.0)
        scale = gain[pl.ds(layer, 1), :] / jnp.sqrt(spread + norm_eps)
        base = shift[pl.ds(layer, 1), :]

        def normalise(block, carry):
            wide = mixed[block].astype(jnp.float32)
            columns[block] = jnp.maximum((wide - centre) * scale + base, 0.0).astype(
                jnp.bfloat16
            )
            return carry

        lax.fori_loop(0, row_count, normalise, 0)

    out_copy = pltpu.make_async_copy(columns.at[pl.ds(0, row_count)], out, out_sem)
    out_copy.start()
    out_copy.wait()


def shards(
    n,
    features,
    tile_values,
    tile_blocks,
    tile_count,
    send_rows,
    recv_index,
    layer_weight,
    norm_gain,
    norm_shift,
):
    tile_total, edge, depth = tile_values.shape
    vertices, channels = features.shape
    row_count = vertices // edge
    layers = layer_weight.shape[0]
    neighbours, halo_count = send_rows.shape[1:]
    group_total = (tile_total + row_count + 1) // 2
    group_total = (group_total + 3) // 4 * 4
    tables = plan(tile_blocks, tile_count[0], row_count, group_total)
    smem = pl.BlockSpec(memory_space=pltpu.SMEM)
    vmem = pl.BlockSpec(memory_space=pltpu.VMEM)
    anywhere = pl.BlockSpec(memory_space=pl.ANY)
    bf16, f32 = jnp.bfloat16, jnp.float32
    result = pl.pallas_call(
        functools.partial(kernel, n),
        out_shape=jax.ShapeDtypeStruct((row_count, edge, channels), bf16),
        in_specs=[smem] * 4 + [vmem] * 5 + [anywhere] * 2,
        out_specs=anywhere,
        scratch_shapes=[
            pltpu.VMEM((tile_total + 1, edge, depth), bf16),
            pltpu.VMEM((row_count + neighbours * halo_count // edge, edge, channels), bf16),
            pltpu.VMEM((neighbours * halo_count, vertices), bf16),
            pltpu.VMEM((neighbours * halo_count, neighbours * halo_count), bf16),
            pltpu.VMEM((group_total, edge, channels), bf16),
            pltpu.VMEM((row_count, edge, channels), bf16),
            pltpu.VMEM((layers, neighbours, halo_count, channels), bf16),
            pltpu.VMEM((layers, neighbours, halo_count, channels), bf16),
            pltpu.VMEM((layers, n, 2, channels), f32),
            pltpu.SemaphoreType.DMA,
            pltpu.SemaphoreType.DMA,
            pltpu.SemaphoreType.DMA,
            pltpu.SemaphoreType.DMA((layers, neighbours)),
            pltpu.SemaphoreType.DMA((layers, neighbours)),
            pltpu.SemaphoreType.DMA((layers, n)),
            pltpu.SemaphoreType.DMA((layers, n)),
        ],
        compiler_params=pltpu.CompilerParams(
            collective_id=0, has_side_effects=True, vmem_limit_bytes=56 * 2**20
        ),
    )(
        *tables,
        send_rows,
        recv_index,
        layer_weight,
        norm_gain,
        norm_shift,
        features.reshape(row_count, edge, channels),
        tile_values,
    )
    return result.reshape(vertices, channels)


def solution(mesh):
    return jax.shard_map(
        functools.partial(shards, mesh.shape["parts"]),
        mesh=mesh,
        in_specs=(
            P("parts", None),
            P("parts", None, None),
            P("parts", None),
            P("parts"),
            P("parts", None, None),
            P("parts", None),
            P(),
            P(),
            P(),
        ),
        out_specs=P("parts", None),
        check_vma=False,
    )
```

time: 389 us -> 73.1 us (0.19)
  matrix products: 190 us -> 0 us
  blocking collectives: 84.7 us -> 0 us
  Pallas kernels: 0 us -> 66.1 us
  local copies, waits for them, and re-layouts: 59.2 us -> 2.26 us
  starting transfers between devices: 22.8 us -> 0 us
  other arithmetic: 16.5 us -> 3.84 us
  waiting for transfers between devices: 12.5 us -> 0 us
    dot_general x34 -> x0, matrix products: 190 us -> none  [the longest x16 126 us: owned_sum(): jnp.einsum('rt,tic->ric', owners.astype(jnp.float32), partial_value, prec...]
    psum x2 -> x0, blocking collectives: 84.7 us -> none  [moments(): lax.psum((jnp.sum(widened, axis=0), jnp.sum(jnp.square(widened), axis=0))...]
    pallas_call x0 -> x1, Pallas kernels: none -> 66.1 us  [shards(): pl.pallas_call(functools.partial(kernel, n), out_shape=jax.ShapeDtypeStru...]
    gather x26 -> x0, local copies, waits for them, and re-layouts: 51.7 us -> none  [the longest x16 33.4 us: owned_sum(): picked = jnp.take(column_blocks, blocks[:, 1], axis=0)]
    ppermute x8 -> x0, starting transfers between devices: 22.8 us -> none  [shifted(): lax.ppermute(value, axis, [(source, source + steps) for source in range(f...]
    ppermute x8 -> x0, waiting for transfers between devices: 12.5 us -> none  [shifted(): lax.ppermute(value, axis, [(source, source + steps) for source in range(f...]
    lt x16 -> x0, other arithmetic: 10.4 us -> none  [owned_sum(): live = tile_number < live_count]
    while x2 -> x0, local copies, waits for them, and re-layouts: 5.46 us -> none  [aggregate(): lax.fori_loop(0, turn_count, one_group, jnp.zeros((row_count, tile_edge,...]
  transfers between devices with their start and end apart: 8 -> 0, of which waited for: 4 -> 0; matrix products, arithmetic and copies ran while one was open for 1% -> 0% of each run, Pallas kernels for 0% -> 0%
where the time goes in v1:
time: 73.1 us; the launch traced here: 72.9 us
  Pallas kernels  66.1 us (90%)
  other arithmetic  3.84 us (5%)
  local copies, waits for them, and re-layouts  2.26 us (3%)
    pallas_call x1, Pallas kernels, shards(): pl.pallas_call(functools.partial(kernel, n), out_shape=jax.ShapeDtypeStru...  66.1 us
    unnamed x1, local copies, waits for them, and re-layouts  2.26 us

profile of v1, /device:TPU:0, one launch (start us, length us, event | category | flops | bytes accessed | tf_op | source)
XLA Modules:
  0.0 72.9 jit_solution(6388897253484872366)
XLA Ops:
  0.7 0.8 %compare_select_fusion = (s32[256,1]{0,1:T(1,128)S(1)}, s32[256,1]{0,1:T(1,128)S(1)}, s32[256,1]{0,1:T(1,128)S(1)}) fusion(s32[]{:T(128)} %bitcast.7, s32[256,2]{0,1:T(2,128)} %param.11), kind=kLoop, calls=%fused_computation.14 | loop fusion | flops 512 | bytes 5124 | tf_op jit(solution)/shard_map/jit(_where)/select_n | solution.py:19
  1.4 0.1 convert_reduce_fusion.2
  1.5 0.2 convert_reduce_fusion
  1.7 0.1 select_reduce_fusion.3
  1.9 0.6 add_add_fusion.last_of
  2.4 0.1 select_reduce_fusion.2
  2.5 0.1 convert_reduce_fusion.1
  2.6 0.6 broadcast_subtract_fusion.keep
  3.2 0.7 %select_reduce_fusion = (s32[272]{0:T(512)}, s32[272]{0:T(512)S(1)}) fusion(s32[256]{0:T(256)S(1)} %bitcast.13, s32[256]{0:T(256)S(1)} %get-tuple-element.11, s32[256]{0:T(256)S(1)} %get-tuple-element.10), kind=kLoop, calls=%fused_computation | loop fusion | flops 347616 | bytes 5248 | tf_op jit(solution)/shard_map/reduce_sum | solution.py:30
  3.9 0.6 broadcast_add_fusion.tile_of
  4.5 66.1 %shard_map.91 = bf16[16,128,256]{2,1,0:T(8,128)(2,1)} custom-call(s32[272]{0:T(512)} %broadcast_add_fusion.tile_of, s32[272]{0:T(512)} %get-tuple-element.5.column_of, f32[136]{0:T(256)} %broadcast_subtract_fusion.keep, s32[16]{0:T(128)} %add_add_fusion.last_of, s32[1,4,256]{2,1,0:T(4,128)} %send_rows.1, s32[1,1024]{1,0:T(1,128)} %recv_index.1, ...), custom_call_target="tpu_custom_call" | custom-call | tf_op jit(solution)/shard_map/pallas_call | solution.py:283
  70.6 2.3 %copy.12 = bf16[2048,256]{1,0:T(8,128)(2,1)} copy(bf16[2048,256]{1,0:T(8,128)(2,1)} %bitcast.9) | data formatting | bytes 2097152
  (3 shorter events, 0.0 us)

commit v2 on v1

v2 whole, which is shorter than its diff:
```python
import functools

import jax
import jax.numpy as jnp
from jax import lax
from jax.experimental import pallas as pl
from jax.experimental.pallas import tpu as pltpu
from jax.sharding import PartitionSpec as P

neighbour_offsets = (1, -1, 2, -2)
norm_eps = 1e-05
MESH = pl.DeviceIdType.MESH


def kernel(
    n,
    tile_count,
    tile_blocks,
    send_rows,
    recv_index,
    weight,
    gain,
    shift,
    features,
    tile_values,
    out,
    affine,
    tiles,
    columns,
    pick,
    order,
    run,
    dense,
    partial,
    mixed,
    outgoing,
    received,
    stats,
    table,
    table_smem,
    tile_sem,
    feature_sem,
    table_sem,
    out_sem,
    halo_send,
    halo_recv,
    stat_send,
    stat_recv,
):
    me = lax.axis_index("parts")
    layers = weight.shape[0]
    tile_total, edge, _ = tile_values.shape
    row_count, _, channels = out.shape
    vertices = row_count * edge
    halo_count = received.shape[2]
    neighbours = len(neighbour_offsets)
    halo_rows = neighbours * halo_count
    column_count = (vertices + halo_rows) // edge
    cell_total = row_count * column_count

    feature_copy = pltpu.make_async_copy(features, columns.at[pl.ds(0, row_count)], feature_sem)
    feature_copy.start()
    tile_copy = pltpu.make_async_copy(tile_values, tiles, tile_sem)
    tile_copy.start()

    barrier = pltpu.get_barrier_semaphore()

    def greet(step, carry):
        pl.semaphore_signal(
            barrier, inc=1, device_id=(lax.rem(me + step, n),), device_id_type=MESH
        )
        return carry

    lax.fori_loop(1, n, greet, 0)

    for position, offset in enumerate(neighbour_offsets):
        source = me - offset

        @pl.when((source < 0) | (source >= n))
        def _():
            for layer in range(layers):
                received[layer, position] = jnp.zeros((halo_count, channels), received.dtype)

    lane = lax.broadcasted_iota(jnp.int32, (128, 128), 1)

    def upright(row):
        return jnp.broadcast_to(row, (128, 128)).T

    def one_hot(index_row, target, first_row, width):
        spread = upright(index_row)
        for chunk in range(width // 128):
            found = spread == lane + chunk * 128
            target[pl.ds(first_row, 128), pl.ds(chunk * 128, 128)] = jnp.where(
                found, 1.0, 0.0
            ).astype(jnp.bfloat16)

    for position in range(neighbours):
        for half in range(halo_count // 128):
            one_hot(
                send_rows[0, pl.ds(position, 1), pl.ds(half * 128, 128)],
                pick,
                position * halo_count + half * 128,
                vertices,
            )
    feature_copy.wait()

    def halo_copy(layer, position, device):
        return pltpu.make_async_remote_copy(
            src_ref=outgoing.at[layer, position],
            dst_ref=received.at[layer, position],
            send_sem=halo_send.at[layer, position],
            recv_sem=halo_recv.at[layer, position],
            device_id=(device,),
            device_id_type=MESH,
        )

    def gather_rows(layer, position):
        outgoing[layer, position] = jnp.dot(
            pick[pl.ds(position * halo_count, halo_count), :],
            columns[pl.ds(0, row_count)].reshape(vertices, channels),
            preferred_element_type=jnp.float32,
        ).astype(jnp.bfloat16)

    def send_halo(layer, position):
        target = me + neighbour_offsets[position]

        @pl.when((target >= 0) & (target < n))
        def _():
            halo_copy(layer, position, target).start()

    count = tile_count[0]
    spans = tile_total // 128
    low = lax.broadcasted_iota(jnp.int32, (1, 128), 1)
    cells, keys = [], []
    for span in range(spans):
        place = pl.ds(span * 128, 128)
        number = low + span * 128
        cell = tile_blocks[pl.ds(0, 1), place] * column_count + tile_blocks[pl.ds(1, 1), place]
        cell = jnp.where(number < count, cell, cell_total)
        cells.append(cell)
        keys.append(cell * tile_total + number)
    tall_cells = [upright(cell) for cell in cells]
    tall_keys = [upright(key) for key in keys]

    def total_over(terms):
        return jnp.sum(functools.reduce(jnp.add, terms), axis=0, keepdims=True)

    def flag(condition):
        return jnp.where(condition, 1, 0)

    slots, repeats = [], []
    for span in range(spans):
        slots.append(total_over([flag(tall < keys[span]) for tall in tall_keys]))
        repeats.append(
            total_over(
                [
                    flag((tall < keys[span]) & (tall_cell == cells[span]))
                    for tall, tall_cell in zip(tall_keys, tall_cells)
                ]
            )
        )
    tall_slots = [upright(slot) for slot in slots]
    tall_repeats = [upright(jnp.minimum(repeat, 1)) for repeat in repeats]
    upward = lax.broadcasted_iota(jnp.int32, (128, 128), 0)
    for span in range(spans):
        here = [tall == low + span * 128 for tall in tall_slots]
        table[pl.ds(0, 1), pl.ds(span * 128, 128)] = total_over(
            [jnp.where(hit, upward + k * 128, 0) for k, hit in enumerate(here)]
        )
        table[pl.ds(0, 1), pl.ds(tile_total + span * 128, 128)] = total_over(
            [jnp.where(hit, tall, 0) for hit, tall in zip(here, tall_repeats)]
        )
    for span in range(cell_total // 128):
        cell = low + span * 128
        reached = total_over([flag(tall <= cell) for tall in tall_cells])
        present = total_over([flag(tall == cell) for tall in tall_cells])
        table[pl.ds(0, 1), pl.ds(2 * tile_total + span * 128, 128)] = jnp.where(
            present > 0, reached - 1, tile_total
        )

    for position in range(neighbours):
        gather_rows(0, position)
    table_copy = pltpu.make_async_copy(table, table_smem, table_sem)
    table_copy.start()
    pl.semaphore_wait(barrier, n - 1)
    for position in range(neighbours):
        send_halo(0, position)
    for part in range(halo_rows // 128):
        one_hot(recv_index[pl.ds(0, 1), pl.ds(part * 128, 128)], order, part * 128, halo_rows)
    table_copy.wait()
    tile_copy.wait()

    run[tile_total] = jnp.zeros((edge, edge), run.dtype)
    unroll = 4

    def sweep(turn, total):
        for step in range(unroll):
            slot = turn * unroll + step
            kept = table_smem[0, tile_total + slot].astype(jnp.float32)
            total = total * kept + tiles[table_smem[0, slot]].astype(jnp.float32)
            run[slot] = total.astype(jnp.bfloat16)
        return total

    lax.fori_loop(0, tile_total // unroll, sweep, jnp.zeros((edge, edge), jnp.float32))

    def lay(block, carry):
        place = pl.ds(pl.multiple_of(block * edge, edge), edge)
        for column in range(column_count):
            dense[place, pl.ds(column * edge, edge)] = run[
                table_smem[0, 2 * tile_total + block * column_count + column]
            ]
        return carry

    lax.fori_loop(0, row_count, lay, 0)

    chunk_rows = 4 * edge if row_count % 4 == 0 else edge
    chunks = vertices // chunk_rows

    for layer in range(layers):
        if layer > 0:
            for position in range(neighbours):
                gather_rows(layer, position)
                send_halo(layer, position)
        for chunk in range(chunks):
            place = pl.ds(chunk * chunk_rows, chunk_rows)
            partial[place, :] = jnp.dot(
                dense[place, pl.ds(0, vertices)],
                columns[pl.ds(0, row_count)].reshape(vertices, channels),
                preferred_element_type=jnp.float32,
            )
        for position, offset in enumerate(neighbour_offsets):
            source = me - offset

            @pl.when((source >= 0) & (source < n))
            def _():
                halo_copy(layer, position, me).wait_recv()

        halo = jnp.dot(
            order[...],
            received[layer].reshape(halo_rows, channels),
            preferred_element_type=jnp.float32,
        ).astype(jnp.bfloat16)
        columns[pl.ds(row_count, halo_rows // edge)] = halo.reshape(
            halo_rows // edge, edge, channels
        )
        sums = jnp.zeros((8, channels), jnp.float32)
        squares = jnp.zeros((8, channels), jnp.float32)
        for chunk in range(chunks):
            place = pl.ds(chunk * chunk_rows, chunk_rows)
            summed = partial[place, :] + jnp.dot(
                dense[place, pl.ds(vertices, halo_rows)],
                columns[pl.ds(row_count, halo_rows // edge)].reshape(halo_rows, channels),
                preferred_element_type=jnp.float32,
            )
            product = jnp.dot(
                summed.astype(jnp.bfloat16), weight[layer], preferred_element_type=jnp.float32
            ).astype(jnp.bfloat16)
            mixed[pl.ds(chunk * chunk_rows // edge, chunk_rows // edge)] = product.reshape(
                chunk_rows // edge, edge, channels
            )
            wide = product.astype(jnp.float32).reshape(chunk_rows // 8, 8, channels)
            sums = sums + jnp.sum(wide, axis=0)
            squares = squares + jnp.sum(wide * wide, axis=0)
        stats[layer, me] = jnp.concatenate(
            [jnp.sum(sums, axis=0, keepdims=True), jnp.sum(squares, axis=0, keepdims=True)], axis=0
        )

        def share(step, carry):
            pltpu.make_async_remote_copy(
                src_ref=stats.at[layer, me],
                dst_ref=stats.at[layer, me],
                send_sem=stat_send.at[layer, step],
                recv_sem=stat_recv.at[layer, step],
                device_id=(lax.rem(me + step, n),),
                device_id_type=MESH,
            ).start()
            return carry

        lax.fori_loop(1, n, share, 0)
        last = layer == layers - 1
        if last:
            out_copy = pltpu.make_async_copy(mixed, out, out_sem)
            out_copy.start()

        for position, offset in enumerate(neighbour_offsets):
            target = me + offset

            @pl.when((target >= 0) & (target < n))
            def _():
                halo_copy(layer, position, target).wait_send()

        def collect(step, carry):
            pltpu.make_async_remote_copy(
                src_ref=stats.at[layer, me],
                dst_ref=stats.at[layer, lax.rem(me + n - step, n)],
                send_sem=stat_send.at[layer, step],
                recv_sem=stat_recv.at[layer, step],
                device_id=(lax.rem(me + step, n),),
                device_id_type=MESH,
            ).wait()
            return carry

        lax.fori_loop(1, n, collect, 0)
        both = jnp.sum(stats[layer], axis=0) / (vertices * n)
        centre = both[0:1]
        spread = jnp.maximum(both[1:2] - centre * centre, 0.0)
        scale = gain[pl.ds(layer, 1), :] / jnp.sqrt(spread + norm_eps)
        base = shift[pl.ds(layer, 1), :]
        if last:
            affine[...] = jnp.concatenate([centre, scale], axis=0)
            out_copy.wait()
        else:
            for block in range(row_count):
                wide = mixed[block].astype(jnp.float32)
                columns[block] = jnp.maximum((wide - centre) * scale + base, 0.0).astype(
                    jnp.bfloat16
                )


def shards(
    n,
    features,
    tile_values,
    tile_blocks,
    tile_count,
    send_rows,
    recv_index,
    layer_weight,
    norm_gain,
    norm_shift,
):
    tile_total, edge, depth = tile_values.shape
    vertices, channels = features.shape
    row_count = vertices // edge
    layers = layer_weight.shape[0]
    neighbours, halo_count = send_rows.shape[1:]
    halo_rows = neighbours * halo_count
    table_size = 2 * tile_total + row_count * (row_count + halo_rows // edge)
    smem = pl.BlockSpec(memory_space=pltpu.SMEM)
    vmem = pl.BlockSpec(memory_space=pltpu.VMEM)
    anywhere = pl.BlockSpec(memory_space=pl.ANY)
    bf16, f32 = jnp.bfloat16, jnp.float32
    mixed, affine = pl.pallas_call(
        functools.partial(kernel, n),
        out_shape=(
            jax.ShapeDtypeStruct((row_count, edge, channels), bf16),
            jax.ShapeDtypeStruct((2, channels), f32),
        ),
        in_specs=[smem] + [vmem] * 6 + [anywhere] * 2,
        out_specs=(anywhere, vmem),
        scratch_shapes=[
            pltpu.VMEM((tile_total, edge, depth), bf16),
            pltpu.VMEM((row_count + halo_rows // edge, edge, channels), bf16),
            pltpu.VMEM((halo_rows, vertices), bf16),
            pltpu.VMEM((halo_rows, halo_rows), bf16),
            pltpu.VMEM((tile_total + 1, edge, depth), bf16),
            pltpu.VMEM((vertices, vertices + halo_rows), bf16),
            pltpu.VMEM((vertices, channels), f32),
            pltpu.VMEM((row_count, edge, channels), bf16),
            pltpu.VMEM((layers, neighbours, halo_count, channels), bf16),
            pltpu.VMEM((layers, neighbours, halo_count, channels), bf16),
            pltpu.VMEM((layers, n, 2, channels), f32),
            pltpu.VMEM((1, table_size), jnp.int32),
            pltpu.SMEM((1, table_size), jnp.int32),
            pltpu.SemaphoreType.DMA,
            pltpu.SemaphoreType.DMA,
            pltpu.SemaphoreType.DMA,
            pltpu.SemaphoreType.DMA,
            pltpu.SemaphoreType.DMA((layers, neighbours)),
            pltpu.SemaphoreType.DMA((layers, neighbours)),
            pltpu.SemaphoreType.DMA((layers, n)),
            pltpu.SemaphoreType.DMA((layers, n)),
        ],
        compiler_params=pltpu.CompilerParams(
            collective_id=0, has_side_effects=True, vmem_limit_bytes=56 * 2**20
        ),
    )(
        tile_count,
        tile_blocks.T,
        send_rows,
        recv_index,
        layer_weight,
        norm_gain,
        norm_shift,
        features.reshape(row_count, edge, channels),
        tile_values,
    )
    wide = mixed.reshape(vertices, channels).astype(f32)
    return jax.nn.relu((wide - affine[0]) * affine[1] + norm_shift[layers - 1]).astype(bf16)


def solution(mesh):
    return jax.shard_map(
        functools.partial(shards, mesh.shape["parts"]),
        mesh=mesh,
        in_specs=(
            P("parts", None),
            P("parts", None, None),
            P("parts", None),
            P("parts"),
            P("parts", None, None),
            P("parts", None),
            P(),
            P(),
            P(),
        ),
        out_specs=P("parts", None),
        check_vma=False,
    )
```

time: 73.1 us -> 52.7 us (0.72)
  Pallas kernels: 66.1 us -> 47.8 us
  other arithmetic: 3.84 us -> 2.59 us
  local copies, waits for them, and re-layouts: 2.26 us -> 1.42 us
    pallas_call x1, Pallas kernels: 66.1 us -> 47.8 us  [shards(): pl.pallas_call(functools.partial(kernel, n), out_shape=(jax.ShapeDtypeStr...]
    convert_element_type x0 -> x1, other arithmetic: none -> 2.59 us  [shards(): jax.nn.relu((wide - affine[0]) * affine[1] + norm_shift[layers - 1])]
    unnamed x1 -> x0, local copies, waits for them, and re-layouts: 2.26 us -> none
    slice x0 -> x2, local copies, waits for them, and re-layouts: none -> 1.42 us  [the longest x1 0.73 us: shards(): affine[0]]
    reduce_sum x6 -> x0, other arithmetic: 1.32 us -> none  [the longest x1 0.73 us: plan(): column_of = jnp.sum(jnp.where(hit, tile_blocks[:, 1][None, :], 0), axis=1)]
    sub x3 -> x0, other arithmetic: 1.16 us -> none  [the longest x1 0.6 us: plan(): 1.0 - jnp.sum((group_number[:, None] == start[None, :]).astype(jnp.float3...]
    select_n x3 -> x0, other arithmetic: 0.78 us -> none  [the longest x2 0.77 us: plan(): rows = jnp.where(live, tile_blocks[:, 0], row_count)]
where the time goes in v2:
time: 52.7 us; the launch traced here: 52.4 us
  Pallas kernels  47.8 us (91%)
  other arithmetic  2.59 us (5%)
  local copies, waits for them, and re-layouts  1.42 us (3%)
  between operations  0.66 us (1%)
    pallas_call x1, Pallas kernels, shards(): pl.pallas_call(functools.partial(kernel, n), out_shape=(jax.ShapeDtypeStr...  47.8 us
    convert_element_type x1, other arithmetic, shards(): jax.nn.relu((wide - affine[0]) * affine[1] + norm_shift[layers - 1])  2.59 us

profile of v2, /device:TPU:0, one launch (start us, length us, event | category | flops | bytes accessed | tf_op | source)
XLA Modules:
  0.0 52.4 jit_solution(6142491264078009688)
XLA Ops:
  0.7 0.7 %slice.11 = f32[1,256]{1,0:T(1,128)S(1)} slice(f32[2,256]{1,0:T(2,128)} %shift.1), slice={[1:2], [0:256]} | slice | bytes 2048 | tf_op jit(solution)/shard_map/slice | solution.py:389
  1.3 47.8 %shard_map.91 = (bf16[16,128,256]{2,1,0:T(8,128)(2,1)}, f32[2,256]{1,0:T(2,128)}) custom-call(s32[1]{0:T(128)S(6)} %copy.10.tile_count, s32[2,256]{1,0:T(2,128)} %bitcast.12, s32[1,4,256]{2,1,0:T(4,128)} %send_rows.1, s32[1,1024]{1,0:T(1,128)} %recv_index.1, bf16[2,256,256]{2,1,0:T(8,128)(2,1)} %weight.1, f32[2,256]{1,0:T(2,128)} %gain.1, f32[2,256]{1,0:T(2,128)} %shift.1, ...), custom_call_target="tpu_custom_call" | custom-call | tf_op jit(solution)/shard_map/pallas_call | solution.py:343
  49.1 0.7 %fusion.4 = (f32[1,256]{1,0:T(1,128)S(1)}, f32[1,256]{1,0:T(1,128)S(1)}) fusion(f32[2,256]{1,0:T(2,128)} %get-tuple-element.8), kind=kLoop, calls=%fused_computation.5 | loop fusion | bytes 4096 | tf_op jit(solution)/shard_map/slice | solution.py:389
  49.8 2.6 %fusion.3 = bf16[2048,256]{1,0:T(8,128)(2,1)} fusion(bf16[16,128,256]{2,1,0:T(8,128)(2,1)} %get-tuple-element.7, f32[256]{0:T(256)S(1)} %bitcast.9, f32[256]{0:T(256)S(1)} %bitcast.11, f32[256]{0:T(256)S(1)} %bitcast.10), kind=kLoop, calls=%fused_computation.4 | loop fusion | flops 3145728 | bytes 2100224 | tf_op jit(solution)/shard_map/convert_element_type | solution.py:389
